TPU v7x, 256 devices: a whole 4x4x8 slice. The times are simulated.
256 devices in a mesh: pb: 16 (over z, core), kv: 16 (over y, x).
Axes of the slice: x: 4, y: 4, z: 8, core: 2. Of those that a mesh axis runs over, the one named last changes fastest.
Arguments:
- queries: bfloat16 [393216, 1024], P(('pb', 'kv')), may hold values from -8 to 8
- keys: bfloat16 [524288, 128], P(('kv', 'pb')), may hold values from -6 to 6
- values: bfloat16 [524288, 128], P(('kv', 'pb')), may hold values from -6 to 6
- selected: int32 [6144, 14], P(('pb', 'kv')), may hold values from 1 to 8190, as said below
Outputs:
- attended: bfloat16 [393216, 1024], P(('pb', 'kv'))
Inputs may be any that keep to these rules, and one draw needn't show every extreme that they name: `selected`: each row names 14 different blocks, never block 0 or block 8191. Key device k holds blocks k * 32 to (k + 1) * 32 - 1, devices counted with kv slowest; query device d holds query blocks d * 24 to (d + 1) * 24 - 1, devices counted with pb slowest. The query blocks of one device name together at most 2 distinct blocks of one key device, and in every draw some key device has exactly 2 named by every query device.
All inputs are finite; a program needn't handle non-finite values.
Results may differ from a plain program's by a relative error of at most 0.0046.
Values may be sent and summed in bfloat16 or wider, within the bound.
A program may use at most 128 MiB of HBM per device.

v0:
```python
import math
import jax
import jax.numpy as jnp
from jax import lax
from jax.sharding import PartitionSpec as P

H = 8
DH = 128
BLOCK = 64
TOPN = 16
QB = 64
CAP = 2


def holdings(wanted, owner, blocks_here):
    local_ids = owner * blocks_here + jnp.arange(blocks_here, dtype=jnp.int32)
    hits = (wanted[:, None] == local_ids[None, :]).astype(jnp.int32)
    present = jnp.max(hits, axis=0)
    return (present, jnp.cumsum(present) - present)


def slot_lists(present, slot_rank, slots):
    local_ids = jnp.arange(present.shape[-1], dtype=jnp.int32)
    slot_ids = jnp.arange(slots, dtype=jnp.int32)
    matches = (present[..., :, None] == 1) & (slot_rank[..., :, None] == slot_ids)
    return jnp.sum(jnp.where(matches, local_ids[:, None], 0), axis=-2)


def per_device(queries, keys, values, selected):
    pb_count = lax.axis_size("pb")
    kv_count = lax.axis_size("kv")
    devices = pb_count * kv_count
    blocks_here = keys.shape[0] // BLOCK
    query_blocks = queries.shape[0] // QB
    column_blocks = pb_count * blocks_here
    tiles_local = jnp.concatenate(
        [keys.reshape(blocks_here, BLOCK, DH), values.reshape(blocks_here, BLOCK, DH)], axis=2
    )
    column = lax.all_gather(tiles_local, "pb", axis=0, tiled=True)
    slots = CAP
    wanted = selected.reshape(-1)
    owners = jnp.arange(devices, dtype=jnp.int32)
    present, slot_rank = jax.vmap(lambda owner: holdings(wanted, owner, blocks_here))(owners)
    owner_lists = slot_lists(present, slot_rank, slots)
    by_column = (
        owner_lists.reshape(kv_count, pb_count, slots)
        + jnp.arange(pb_count, dtype=jnp.int32)[None, :, None] * blocks_here
    )
    by_column = by_column.reshape(kv_count, pb_count * slots)
    asked_for = lax.all_to_all(by_column, "kv", split_axis=0, concat_axis=0, tiled=True)
    outgoing = jnp.take(column, asked_for.reshape(-1), axis=0).reshape(
        kv_count, pb_count * slots, BLOCK, 2 * DH
    )
    fetched = lax.all_to_all(outgoing, "kv", split_axis=0, concat_axis=0, tiled=True)
    tile_table = fetched.reshape(devices * slots, BLOCK, 2 * DH)
    owner_of = selected // blocks_here
    positions = owner_of * slots + jnp.take(slot_rank.reshape(-1), selected)
    me_kv = lax.axis_index("kv")
    ends = jnp.concatenate([column[:1], column[column_blocks - 1 :]], axis=0)
    ends = jnp.where(
        jnp.stack([me_kv == 0, me_kv == kv_count - 1])[:, None, None], ends, jnp.zeros_like(ends)
    )
    ends = lax.psum(ends, "kv")
    tile_table = jnp.concatenate([tile_table, ends], axis=0)
    extra_base = devices * slots
    leading_positions = jnp.broadcast_to(
        jnp.array([extra_base, extra_base + 1], jnp.int32), (query_blocks, 2)
    )
    positions = jnp.concatenate([leading_positions, positions], axis=1)
    group_size = math.gcd(query_blocks, 8)
    q_groups = queries.reshape(query_blocks // group_size, group_size, QB * H, DH)
    p_groups = positions.reshape(query_blocks // group_size, group_size, TOPN)

    def attend(operands):
        q_block, positions_in = operands
        gathered = jnp.take(tile_table, positions_in.reshape(-1), axis=0).reshape(
            group_size, TOPN * BLOCK, 2 * DH
        )
        scores = jnp.einsum(
            "gqd,gkd->gqk", q_block, gathered[..., :DH], preferred_element_type=jnp.float32
        ) * DH ** (-0.5)
        weights = jnp.exp(scores - jnp.max(scores, axis=-1, keepdims=True))
        totals = jnp.sum(weights, axis=-1, keepdims=True)
        weighted = jnp.einsum(
            "gqk,gkd->gqd",
            weights.astype(jnp.bfloat16),
            gathered[..., DH:],
            preferred_element_type=jnp.float32,
        )
        return (weighted / totals).astype(jnp.bfloat16)

    result = lax.map(attend, (q_groups, p_groups))
    return result.reshape(query_blocks * QB, H * DH)


def solution(mesh):
    placed = (
        P(("pb", "kv"), None),
        P(("kv", "pb"), None),
        P(("kv", "pb"), None),
        P(("pb", "kv"), None),
    )
    return jax.shard_map(
        per_device, mesh=mesh, in_specs=placed, out_specs=P(("pb", "kv"), None), check_vma=False
    )
```

profile of v0, /device:TPU:2, one launch (start us, length us, event | category | flops | bytes accessed | tf_op | source)
XLA Modules:
  0.0 519.4 jit_solution(11960891043452149832)
XLA Ops:
  6.5 0.0 all-gather.2.cloned.1.call-start
  6.5 2.3 pad_maximum_fusion.1
  8.9 0.0 all-gather.2.cloned.1.call-update
  8.9 0.1 add.104
  9.0 0.1 add.105
  9.0 0.8 copy.30
  9.8 0.1 eq.45
  9.9 1.7 convert_reduce_fusion
  11.7 0.1 reduce_window_sum.11
  11.8 0.1 copy.38
  11.9 0.1 reshape.205
  12.1 13.5 %all_to_all.11 = s32[16,1,32]{2,1,0:T(1,128)S(1)} all-to-all(s32[16,1,32]{2,1,0:T(1,128)S(1)} %bitcast.44), channel_id=1, replica_groups=mesh['pb'=16,'kv'=16] {'kv'}, dimensions={0} | all-to-all | bytes 4096 | tf_op jit(solution)/shard_map/all_to_all | solution.py:50
  25.5 0.5 broadcast.157
  26.0 0.6 reduce.3
  26.6 0.1 reshape.209
  26.7 80.8 %all-gather.2.cloned.1.call-done = bf16[512,64,256]{2,1,0:T(8,128)(2,1)} async-done(((bf16[32,64,256]{2,1,0:T(8,128)(2,1)}), bf16[512,64,256]{2,1,0:T(8,128)(2,1)}) %all-gather.2.cloned.1.call-update) | async-done | bytes 16777232 | tf_op jit(solution)/shard_map/all_gather | solution.py:39
  107.6 19.5 %gather_fusion.2 = bf16[512,64,256]{2,1,0:T(8,128)(2,1)} fusion(bf16[512,64,256]{2,1,0:T(8,128)(2,1)} %all-gather.2.cloned.1.call-done, s32[1024]{0:T(1024)S(1)} %pad_clamp_fusion.1), kind=kCustom, calls=%fused_computation.2 | custom fusion | bytes 33556480 | tf_op jit(solution)/shard_map/jit(_take)/gather | solution.py:51
  127.0 14.1 %broadcast_select_fusion = bf16[16,32,64,256]{3,2,1,0:T(8,128)(2,1)} fusion(bf16[16,32,64,256]{3,2,1,0:T(8,128)(2,1)} %bitcast.40, pred[16,32]{1,0:T(8,128)(4,1)S(1)} %compare_and_fusion.1), kind=kLoop, calls=%fused_computation.27 | loop fusion | flops 8388608 | bytes 33554944 | tf_op jit(solution)/shard_map/jit(_take)/select_n | solution.py:51
  141.2 0.0 copy-start
  141.2 7.4 %all-to-all-start.1 = ((bf16[16,32,64,256]{3,2,1,0:T(8,128)(2,1)}), bf16[16,32,64,256]{3,2,1,0:T(8,128)(2,1)}, u32[]{:S(2)}, u32[]{:S(2)}) async-start(bf16[16,32,64,256]{3,2,1,0:T(8,128)(2,1)} %broadcast_select_fusion), calls=%async_computation.1 | async-start | bytes 33554432 | tf_op jit(solution)/shard_map/all_to_all | solution.py:54
  148.6 0.0 all-reduce.2.cloned.1.call-start
  148.6 0.1 copy.37
  148.7 0.0 copy-done
  148.8 0.1 reshape.222
  148.9 0.1 sub.27
  149.0 2.5 gather_fusion.1
  151.5 0.1 reshape.221
  151.6 0.1 pad_add_fusion
  151.7 0.8 fusion.23
  152.5 0.7 maximum_select_fusion
  153.2 0.0 all-reduce.2.cloned.1.call-update
  153.2 0.1 add_bitcast_fusion
  153.3 4.1 reshape.203
  157.4 264.4 %all-reduce.2.cloned.1.call-done = bf16[2,64,256]{2,1,0:T(8,128)(2,1)} async-done(((bf16[2,64,256]{2,1,0:T(8,128)(2,1)}), bf16[2,64,256]{2,1,0:T(8,128)(2,1)}) %all-reduce.2.cloned.1.call-update) | async-done | bytes 65552 | tf_op jit(solution)/shard_map/psum | solution.py:63
  421.9 0.0 all-to-all-done.1
  421.9 14.1 %pad_maximum_fusion = bf16[514,64,256]{2,1,0:T(8,128)(2,1)} fusion(bf16[2,64,256]{2,1,0:T(8,128)(2,1)} %all-reduce.2.cloned.1.call-done, bf16[512,64,256]{2,1,0:T(8,128)(2,1)} %bitcast.12), kind=kLoop, calls=%fused_computation.26 | loop fusion | flops 8421376 | bytes 33685504 | tf_op jit(solution)/shard_map/concatenate | solution.py:64
  436.0 70.9 %while.10 = (s32[]{:T(128)}, bf16[3,8,512,128]{3,2,1,0:T(8,128)(2,1)}, bf16[3,8,512,128]{3,2,1,0:T(8,128)(2,1)S(1)}, s32[3,8,16]{2,1,0:T(8,128)S(1)}, bf16[514,64,256]{2,1,0:T(8,128)(2,1)}, /*index=5*/s32[]{:T(128)}) while((s32[]{:T(128)}, bf16[3,8,512,128]{3,2,1,0:T(8,128)(2,1)}, bf16[3,8,512,128]{3,2,1,0:T(8,128)(2,1)S(1)}, ...), condition=%wide.region_7.8_spmd, body=%wide.region_4.7_spmd.sunk | while | flops 2184177664 | bytes 73523544 | solution.py:92
  436.0 0.1 reshape.253
  436.1 0.1 broadcast_in_dim.101
  436.2 0.1 broadcast_in_dim.102
  436.3 8.5 %gather_fusion = bf16[128,64,256]{2,1,0:T(8,128)(2,1)} fusion(bf16[514,64,256]{2,1,0:T(8,128)(2,1)} %get-tuple-element.104, s32[1024]{0:T(1024)S(1)} %pad_clamp_fusion.4), kind=kCustom, calls=%fused_computation.clone.1 | custom fusion | bytes 8389120 | tf_op jit(solution)/shard_map/while/body/eval_jaxpr/jit(_take)/gather | solution.py:76
  444.8 4.6 bitcast_select_fusion.2
  449.4 2.4 multiply_reduce_fusion.2
  451.8 3.5 fusion.31
  455.3 4.2 bitcast_dynamic-update-slice_fusion.2
  459.6 0.1 reshape.253
  459.7 0.1 broadcast_in_dim.101
  459.8 0.1 broadcast_in_dim.102
  459.9 8.5 %gather_fusion = bf16[128,64,256]{2,1,0:T(8,128)(2,1)} fusion(bf16[514,64,256]{2,1,0:T(8,128)(2,1)} %get-tuple-element.104, s32[1024]{0:T(1024)S(1)} %pad_clamp_fusion.4), kind=kCustom, calls=%fused_computation.clone.1 | custom fusion | bytes 8389120 | tf_op jit(solution)/shard_map/while/body/eval_jaxpr/jit(_take)/gather | solution.py:76
  468.4 4.6 bitcast_select_fusion.2
  473.0 2.4 multiply_reduce_fusion.2
  475.4 3.5 fusion.31
  479.0 4.2 bitcast_dynamic-update-slice_fusion.2
  483.2 0.1 reshape.253
  483.3 0.1 broadcast_in_dim.101
  483.4 0.1 broadcast_in_dim.102
  483.5 8.5 %gather_fusion = bf16[128,64,256]{2,1,0:T(8,128)(2,1)} fusion(bf16[514,64,256]{2,1,0:T(8,128)(2,1)} %get-tuple-element.104, s32[1024]{0:T(1024)S(1)} %pad_clamp_fusion.4), kind=kCustom, calls=%fused_computation.clone.1 | custom fusion | bytes 8389120 | tf_op jit(solution)/shard_map/while/body/eval_jaxpr/jit(_take)/gather | solution.py:76
  492.0 4.6 bitcast_select_fusion.2
  496.6 2.4 multiply_reduce_fusion.2
  499.0 3.5 fusion.31
  502.6 4.2 bitcast_dynamic-update-slice_fusion.2
  506.8 5.8 %reshape.211 = bf16[1536,1024]{1,0:T(8,128)(2,1)} reshape(bf16[3,8,512,128]{3,2,1,0:T(8,128)(2,1)} %get-tuple-element.32) | data formatting | bytes 6291456 | tf_op jit(solution)/shard_map/reshape | solution.py:93
  (24 shorter events, 0.2 us)
Async XLA Ops:
  6.5 101.0 %all-gather.2.cloned.1.call-start = ((), (), s32[]{:S(2)}) async-start(), calls=%async_computation.2 | async-start | bytes 17825792 | tf_op jit(solution)/shard_map/all_gather | solution.py:39
  141.2 7.5 %copy-start = (s32[2]{0:T(128)S(1)}, s32[2]{0:T(128)}, u32[]{:S(2)}) copy-start(s32[2]{0:T(128)} %constant.100.clone) | copy-start | bytes 28
  141.2 280.7 %all-to-all-start.1 = ((bf16[16,32,64,256]{3,2,1,0:T(8,128)(2,1)}), bf16[16,32,64,256]{3,2,1,0:T(8,128)(2,1)}, u32[]{:S(2)}, u32[]{:S(2)}) async-start(bf16[16,32,64,256]{3,2,1,0:T(8,128)(2,1)} %broadcast_select_fusion), calls=%async_computation.1 | async-start | bytes 33554432 | tf_op jit(solution)/shard_map/all_to_all | solution.py:54
  148.6 273.3 %all-reduce.2.cloned.1.call-start = ((), (), s32[]{:S(2)}) async-start(), calls=%async_computation.3 | async-start | bytes 131072 | tf_op jit(solution)/shard_map/psum | solution.py:63
Sparse Core Ops, SparseCore 0:
  9.2 98.3 all-gather.1
  153.3 268.4 all-reduce.1
where the time goes:
time: 521 us; the launch traced here: 519 us
  waiting for transfers between devices  345 us (66%)
  local copies, waits for them, and re-layouts  61.3 us (12%)
  other arithmetic  58.3 us (11%)
  matrix products  20 us (4%)
  between operations  13.6 us (3%)
  blocking collectives  13.5 us (3%)
  starting transfers between devices  7.43 us (1%)
    psum x1, waiting for transfers between devices, per_device(): ends = lax.psum(ends, 'kv')  264 us
    all_gather x1, waiting for transfers between devices, per_device(): column = lax.all_gather(tiles_local, 'pb', axis=0, tiled=True)  80.8 us
    gather x3, local copies, waits for them, and re-layouts, attend(): jnp.take(tile_table, positions_in.reshape(-1), axis=0)  25.6 us
    gather x1, local copies, waits for them, and re-layouts, per_device(): jnp.take(column, asked_for.reshape(-1), axis=0)  19.5 us
    select_n x2, other arithmetic, per_device(): jnp.take(column, asked_for.reshape(-1), axis=0)  14.1 us
    concatenate x1, other arithmetic, per_device(): tile_table = jnp.concatenate([tile_table, ends], axis=0)  14.1 us
    select_n x6, other arithmetic, attend(): jnp.take(tile_table, positions_in.reshape(-1), axis=0)  13.7 us
    all_to_all x1, blocking collectives, per_device(): lax.all_to_all(by_column, 'kv', split_axis=0, concat_axis=0, tiled=True)  13.5 us
  transfers between devices with their start and end apart: 3, of which 2 were waited for; matrix products, arithmetic and copies ran while one was open for 3% of the time, Pallas kernels for 0%

commit v1 on v0

--- a/solution.py
+++ b/solution.py
@@ -1,3 +1,4 @@
+import functools
 import math
 import jax
 import jax.numpy as jnp
@@ -10,6 +11,19 @@
 TOPN = 16
 QB = 64
 CAP = 2
+
+
+def start_strips_all(vals, ndim_at):
+    new = lax.all_to_all(
+        jnp.stack([vals for _ in range(lax.axis_size("pb"))]),
+        axis_name="pb",
+        split_axis=0,
+        concat_axis=0,
+    )
+    return jnp.concatenate(new, axis=ndim_at)
+
+
+map_save = functools.partial(start_strips_all, ndim_at=0)
 
 
 def holdings(wanted, owner, blocks_here):
@@ -36,7 +50,7 @@
     tiles_local = jnp.concatenate(
         [keys.reshape(blocks_here, BLOCK, DH), values.reshape(blocks_here, BLOCK, DH)], axis=2
     )
-    column = lax.all_gather(tiles_local, "pb", axis=0, tiled=True)
+    column = map_save(tiles_local)
     slots = CAP
     wanted = selected.reshape(-1)
     owners = jnp.arange(devices, dtype=jnp.int32)

time: 521 us -> 816 us (1.57)
  waiting for transfers between devices: 345 us -> 633 us
  starting transfers between devices: 7.43 us -> 22.6 us
  blocking collectives: 13.5 us -> 0 us
    all_to_all x0 -> x2, waiting for transfers between devices: none -> 367 us  [the longest x1 363 us: start_strips_all(): lax.all_to_all(jnp.stack([vals for _ in range(lax.axis_size('pb'))]), axi...]
    all_gather x1 -> x0, waiting for transfers between devices: 80.8 us -> none  [per_device(): column = lax.all_gather(tiles_local, 'pb', axis=0, tiled=True)]
    all_to_all x0 -> x2, starting transfers between devices: none -> 16.1 us  [the longest x1 8.62 us: start_strips_all(): lax.all_to_all(jnp.stack([vals for _ in range(lax.axis_size('pb'))]), axi...]
    all_to_all x1 -> x0, blocking collectives: 13.5 us -> none  [per_device(): lax.all_to_all(by_column, 'kv', split_axis=0, concat_axis=0, tiled=True)]
  transfers between devices with their start and end apart: 3 -> 4, of which waited for: 2 -> 3; matrix products, arithmetic and copies ran while one was open for 3% -> 1% of each run, Pallas kernels for 0% -> 0%
where the time goes in v1:
time: 816 us; the launch traced here: 815 us
  waiting for transfers between devices  633 us (78%)
  local copies, waits for them, and re-layouts  67.3 us (8%)
  other arithmetic  58 us (7%)
  starting transfers between devices  22.6 us (3%)
  matrix products  20 us (2%)
  between operations  13.6 us (2%)
    all_to_all x1, waiting for transfers between devices, start_strips_all(): lax.all_to_all(jnp.stack([vals for _ in range(lax.axis_size('pb'))]), axi...  363 us
    psum x1, waiting for transfers between devices, per_device(): ends = lax.psum(ends, 'kv')  266 us
    gather x3, local copies, waits for them, and re-layouts, attend(): jnp.take(tile_table, positions_in.reshape(-1), axis=0)  25.6 us
    gather x1, local copies, waits for them, and re-layouts, per_device(): jnp.take(column, asked_for.reshape(-1), axis=0)  19.5 us
  transfers between devices with their start and end apart: 4, of which 3 were waited for; matrix products, arithmetic and copies ran while one was open for 1% of the time, Pallas kernels for 0%

profile of v1, /device:TPU:2, one launch (start us, length us, event | category | flops | bytes accessed | tf_op | source)
XLA Modules:
  0.0 814.7 jit_solution(3307979428406778152)
XLA Ops:
  6.5 0.1 add.104
  6.6 0.1 add.105
  6.7 0.8 copy.30
  7.5 0.1 eq.45
  7.6 1.7 convert_reduce_fusion
  9.3 0.1 reduce_window_sum.11
  9.4 0.1 copy.38
  9.6 0.1 reshape.210
  9.7 0.6 broadcast_add_fusion
  10.3 7.5 all-to-all-start
  17.8 1.3 pad_maximum_fusion.1
  19.1 4.8 all-to-all-done
  23.9 5.9 stack.8
  29.8 8.6 %all-to-all-start.1 = ((bf16[16,32,64,256]{3,2,1,0:T(8,128)(2,1)}), bf16[16,32,64,256]{3,2,1,0:T(8,128)(2,1)}, u32[]{:S(2)}, u32[]{:S(2)}) async-start(bf16[16,32,64,256]{3,2,1,0:T(8,128)(2,1)} %stack.8), calls=%async_computation.1 | async-start | bytes 33554432 | tf_op jit(solution)/shard_map/all_to_all | solution.py:17
  38.5 0.5 broadcast.159
  39.0 0.7 reduce.3
  39.7 0.1 reshape.215
  39.8 362.7 %all-to-all-done.1 = bf16[16,32,64,256]{3,2,1,0:T(8,128)(2,1)} async-done(((bf16[16,32,64,256]{3,2,1,0:T(8,128)(2,1)}), bf16[16,32,64,256]{3,2,1,0:T(8,128)(2,1)}, u32[]{:S(2)}, u32[]{:S(2)}) %all-to-all-start.1) | async-done | bytes 16777248 | tf_op jit(solution)/shard_map/all_to_all | solution.py:17
  402.4 19.5 %gather_fusion.2 = bf16[512,64,256]{2,1,0:T(8,128)(2,1)} fusion(bf16[512,64,256]{2,1,0:T(8,128)(2,1)} %bitcast.10, s32[1024]{0:T(1024)S(1)} %pad_clamp_fusion.1), kind=kCustom, calls=%fused_computation.2 | custom fusion | bytes 33556480 | tf_op jit(solution)/shard_map/jit(_take)/gather | solution.py:65
  421.9 14.1 %broadcast_select_fusion = bf16[16,32,64,256]{3,2,1,0:T(8,128)(2,1)} fusion(bf16[16,32,64,256]{3,2,1,0:T(8,128)(2,1)} %bitcast.41, pred[16,32]{1,0:T(8,128)(4,1)S(1)} %compare_and_fusion.1), kind=kLoop, calls=%fused_computation.27 | loop fusion | flops 8388608 | bytes 33554944 | tf_op jit(solution)/shard_map/jit(_take)/select_n | solution.py:65
  436.0 0.0 copy-start
  436.0 6.5 all-to-all-start.2
  442.5 0.0 all-reduce.2.cloned.1.call-start
  442.6 0.1 copy.37
  442.7 0.0 copy-done
  442.7 0.1 reshape.228
  442.8 0.1 sub.27
  442.9 2.5 gather_fusion.1
  445.5 0.1 reshape.227
  445.5 0.1 pad_add_fusion
  445.6 0.8 fusion.23
  446.4 0.7 maximum_select_fusion
  447.1 0.0 all-reduce.2.cloned.1.call-update
  447.2 0.1 add_bitcast_fusion
  447.2 4.1 reshape.208
  451.4 265.7 %all-reduce.2.cloned.1.call-done = bf16[2,64,256]{2,1,0:T(8,128)(2,1)} async-done(((bf16[2,64,256]{2,1,0:T(8,128)(2,1)}), bf16[2,64,256]{2,1,0:T(8,128)(2,1)}) %all-reduce.2.cloned.1.call-update) | async-done | bytes 65552 | tf_op jit(solution)/shard_map/psum | solution.py:77
  717.1 0.0 all-to-all-done.2
  717.1 14.1 %pad_maximum_fusion = bf16[514,64,256]{2,1,0:T(8,128)(2,1)} fusion(bf16[2,64,256]{2,1,0:T(8,128)(2,1)} %all-reduce.2.cloned.1.call-done, bf16[512,64,256]{2,1,0:T(8,128)(2,1)} %bitcast.13), kind=kLoop, calls=%fused_computation.26 | loop fusion | flops 8421376 | bytes 33685504 | tf_op jit(solution)/shard_map/concatenate | solution.py:78
  731.2 70.9 %while.10 = (s32[]{:T(128)}, bf16[3,8,512,128]{3,2,1,0:T(8,128)(2,1)}, bf16[3,8,512,128]{3,2,1,0:T(8,128)(2,1)S(1)}, s32[3,8,16]{2,1,0:T(8,128)S(1)}, bf16[514,64,256]{2,1,0:T(8,128)(2,1)}, /*index=5*/s32[]{:T(128)}) while((s32[]{:T(128)}, bf16[3,8,512,128]{3,2,1,0:T(8,128)(2,1)}, bf16[3,8,512,128]{3,2,1,0:T(8,128)(2,1)S(1)}, ...), condition=%wide.region_7.8_spmd, body=%wide.region_4.7_spmd.sunk | while | flops 2184177664 | bytes 73523544 | solution.py:106
  731.2 0.1 reshape.259
  731.3 0.1 broadcast_in_dim.101
  731.4 0.1 broadcast_in_dim.102
  731.5 8.5 %gather_fusion = bf16[128,64,256]{2,1,0:T(8,128)(2,1)} fusion(bf16[514,64,256]{2,1,0:T(8,128)(2,1)} %get-tuple-element.104, s32[1024]{0:T(1024)S(1)} %pad_clamp_fusion.4), kind=kCustom, calls=%fused_computation.clone.1 | custom fusion | bytes 8389120 | tf_op jit(solution)/shard_map/while/body/eval_jaxpr/jit(_take)/gather | solution.py:90
  740.1 4.6 bitcast_select_fusion.2
  744.6 2.4 multiply_reduce_fusion.2
  747.0 3.5 fusion.31
  750.6 4.2 bitcast_dynamic-update-slice_fusion.2
  754.8 0.1 reshape.259
  754.9 0.1 broadcast_in_dim.101
  755.0 0.1 broadcast_in_dim.102
  755.1 8.5 %gather_fusion = bf16[128,64,256]{2,1,0:T(8,128)(2,1)} fusion(bf16[514,64,256]{2,1,0:T(8,128)(2,1)} %get-tuple-element.104, s32[1024]{0:T(1024)S(1)} %pad_clamp_fusion.4), kind=kCustom, calls=%fused_computation.clone.1 | custom fusion | bytes 8389120 | tf_op jit(solution)/shard_map/while/body/eval_jaxpr/jit(_take)/gather | solution.py:90
  763.7 4.6 bitcast_select_fusion.2
  768.2 2.4 multiply_reduce_fusion.2
  770.7 3.5 fusion.31
  774.2 4.2 bitcast_dynamic-update-slice_fusion.2
  778.5 0.1 reshape.259
  778.6 0.1 broadcast_in_dim.101
  778.6 0.1 broadcast_in_dim.102
  778.7 8.5 %gather_fusion = bf16[128,64,256]{2,1,0:T(8,128)(2,1)} fusion(bf16[514,64,256]{2,1,0:T(8,128)(2,1)} %get-tuple-element.104, s32[1024]{0:T(1024)S(1)} %pad_clamp_fusion.4), kind=kCustom, calls=%fused_computation.clone.1 | custom fusion | bytes 8389120 | tf_op jit(solution)/shard_map/while/body/eval_jaxpr/jit(_take)/gather | solution.py:90
  787.3 4.6 bitcast_select_fusion.2
  791.9 2.4 multiply_reduce_fusion.2
  794.3 3.5 fusion.31
  797.8 4.2 bitcast_dynamic-update-slice_fusion.2
  802.1 5.8 reshape.217
  (23 shorter events, 0.2 us)
Async XLA Ops:
  10.3 13.6 %all-to-all-start = ((s32[16,1,32]{2,1,0:T(1,128)}), s32[16,1,32]{2,1,0:T(1,128)S(1)}, u32[]{:S(2)}, u32[]{:S(2)}) async-start(s32[16,1,32]{2,1,0:T(1,128)} %bitcast.6), calls=%async_computation | async-start | bytes 16384 | tf_op jit(solution)/shard_map/all_to_all | solution.py:64
  29.8 372.6 %all-to-all-start.1 = ((bf16[16,32,64,256]{3,2,1,0:T(8,128)(2,1)}), bf16[16,32,64,256]{3,2,1,0:T(8,128)(2,1)}, u32[]{:S(2)}, u32[]{:S(2)}) async-start(bf16[16,32,64,256]{3,2,1,0:T(8,128)(2,1)} %stack.8), calls=%async_computation.1 | async-start | bytes 33554432 | tf_op jit(solution)/shard_map/all_to_all | solution.py:17
  436.0 6.6 copy-start
  436.0 281.1 %all-to-all-start.2 = ((bf16[16,32,64,256]{3,2,1,0:T(8,128)(2,1)}), bf16[16,32,64,256]{3,2,1,0:T(8,128)(2,1)}, u32[]{:S(2)}, u32[]{:S(2)}) async-start(bf16[16,32,64,256]{3,2,1,0:T(8,128)(2,1)} %broadcast_select_fusion), calls=%async_computation.2 | async-start | bytes 33554432 | tf_op jit(solution)/shard_map/all_to_all | solution.py:68
  442.5 274.6 %all-reduce.2.cloned.1.call-start = ((), (), s32[]{:S(2)}) async-start(), calls=%async_computation.3 | async-start | bytes 131072 | tf_op jit(solution)/shard_map/psum | solution.py:77
Sparse Core Ops, SparseCore 0:
  447.3 269.7 all-reduce.1
